TPU v7x, 256 devices: a whole 4x4x8 slice. The times are simulated.
256 devices in a mesh: tile: 64 (over z, x, core), mem: 4 (over y).
Axes of the slice: x: 4, y: 4, z: 8, core: 2. Of those that a mesh axis runs over, the one named last changes fastest.
Arguments:
- footprints: bfloat16 [8192, 128, 128], P('tile'), may hold values from -0.1875 to 0.1875
- tile_row: int32 [8192], P('tile'), may hold values from 0 to 1023, as said below
- tile_col: int32 [8192], P('tile'), may hold values from 0 to 511, as said below
- prior_flux: bfloat16 [256, 65536], P('mem', 'tile'), may hold values from -12 to 12
- observed: float32 [256, 131072], P('mem', 'tile'), may hold values from -6 to 6
- precision_weight: int32 [131072], P('tile'), may hold values from 1 to 16
Outputs:
- gradient: float32 [256, 65536], P('mem', 'tile')
Inputs may be any that keep to these rules, and one draw needn't show every extreme that they name: Among the 128 tiles of each index of tile, at most 3 have a row block of one owner (owner = tile_row // 16); in every draw one owner gets exactly 3 from every index. Likewise with owner = tile_col // 8: at most 3 from one index of tile to one owner, and one owner gets exactly 3 from every index.
All inputs are finite; a program needn't handle non-finite values.
Results may differ from a plain program's by a relative error of at most 0.0052.
Values may be sent and summed in bfloat16 or wider, within the bound.
A program may use at most 64 MiB of HBM per device.

v0:
```python
import jax
import jax.numpy as jnp
from jax import lax
from jax.sharding import PartitionSpec as P

MEMBERS = 256
FLUX_DEV = 8
SOUND_DEV = 16


def sent_to_all(value, axis):
    size = lax.axis_size(axis)
    return lax.all_to_all(
        jnp.broadcast_to(value[None], (size, *value.shape)), axis, 0, 0, tiled=True
    )


def over_copies(value, axis):
    return sent_to_all(value, axis).sum(axis=0)


def slot_of(owners, capacity):
    entries = owners.shape[0]
    position = jnp.arange(entries)
    earlier = (owners[:, None] == owners[None, :]) & (position[None, :] < position[:, None])
    return owners * capacity + jnp.sum(earlier.astype(jnp.int32), axis=1)


def invert(slot_ids, slot_total):
    matches = slot_ids[None, :] == jnp.arange(slot_total)[:, None]
    sources = jnp.sum(jnp.where(matches, jnp.arange(slot_ids.shape[0])[None, :], 0), axis=1)
    return (sources, jnp.any(matches, axis=1))


def to_slots(values, sources, usage_flags):
    placed = jnp.take(values, sources, axis=1)
    return jnp.where(usage_flags[None, :, None], placed, jnp.zeros_like(placed))


def body(footprints, tile_row, tile_col, prior_flux, observed, precision_weight):
    devices_tile = lax.axis_size("tile")
    tile_count = footprints.shape[0]
    tile_size = footprints.shape[1]
    capacity = tile_count // devices_tile + max(1, tile_count // (2 * devices_tile))
    slot_total = devices_tile * capacity
    local_members = prior_flux.shape[0]
    local_sum = jnp.sum(prior_flux.astype(jnp.float32), axis=0)
    ensemble_sum = over_copies(local_sum, "mem")
    ensemble_mean = ensemble_sum / MEMBERS
    member_deviations = (prior_flux.astype(jnp.float32) - ensemble_mean[None, :]).astype(
        jnp.bfloat16
    )
    row_owner = tile_row // SOUND_DEV
    row_local = tile_row % SOUND_DEV
    col_owner = tile_col // FLUX_DEV
    col_local = tile_col % FLUX_DEV
    row_slot = slot_of(row_owner, capacity)
    col_slot = slot_of(col_owner, capacity)
    row_source, row_used = invert(row_slot, slot_total)
    col_source, col_used = invert(col_slot, slot_total)
    gathered = lax.all_gather(member_deviations, "tile", axis=1, tiled=True)
    retrieved_blocks = jnp.take(gathered.reshape(local_members, -1, tile_size), tile_col, axis=1)
    forward_terms = jnp.einsum(
        "mtk,trk->mtr", retrieved_blocks, footprints, preferred_element_type=jnp.float32
    )
    row_index = jnp.where(row_used, jnp.take(row_local, row_source), SOUND_DEV)
    sent_terms = to_slots(forward_terms, row_source, row_used)
    got_terms, got_rows = (
        lax.all_to_all(
            sent_terms.astype(jnp.bfloat16), "tile", split_axis=1, concat_axis=1, tiled=True
        ).astype(sent_terms.dtype),
        lax.all_to_all(row_index[None, :], "tile", split_axis=1, concat_axis=1, tiled=True),
    )
    got_rows = got_rows[0]
    row_match = (got_rows[None, :] == jnp.arange(SOUND_DEV)[:, None]).astype(jnp.float32)
    modelled = jnp.einsum("ds,msk->mdk", row_match, got_terms, precision=lax.Precision.HIGHEST)
    targets = observed.reshape(local_members, SOUND_DEV, tile_size)
    obs_weight = (precision_weight.astype(jnp.float32) / 8.0).reshape(SOUND_DEV, tile_size)
    weighted = (obs_weight[None, :, :] * (modelled - targets)).astype(jnp.bfloat16)
    reply_rows = jnp.take(weighted, jnp.minimum(got_rows, SOUND_DEV - 1), axis=1)
    returned = lax.all_to_all(reply_rows, "tile", split_axis=1, concat_axis=1, tiled=True)
    residual_tiles = jnp.take(returned, row_slot, axis=1)
    backward_terms = jnp.einsum(
        "mtr,trk->mtk", residual_tiles, footprints, preferred_element_type=jnp.float32
    )
    col_index = jnp.where(col_used, jnp.take(col_local, col_source), FLUX_DEV)
    sent_back = to_slots(backward_terms, col_source, col_used)
    got_back, got_cols = (
        lax.all_to_all(
            sent_back.astype(jnp.bfloat16), "tile", split_axis=1, concat_axis=1, tiled=True
        ).astype(sent_back.dtype),
        lax.all_to_all(col_index[None, :], "tile", split_axis=1, concat_axis=1, tiled=True),
    )
    col_match = (got_cols[0][None, :] == jnp.arange(FLUX_DEV)[:, None]).astype(jnp.float32)
    reduced_total = jnp.einsum("fs,msk->mfk", col_match, got_back, precision=lax.Precision.HIGHEST)
    gradient = reduced_total.reshape(local_members, FLUX_DEV * tile_size)
    return gradient


def solution(mesh):
    in_specs = (
        P("tile", None, None),
        P("tile"),
        P("tile"),
        P("mem", "tile"),
        P("mem", "tile"),
        P("tile"),
    )
    out_specs = P("mem", "tile")
    return jax.shard_map(body, mesh=mesh, in_specs=in_specs, out_specs=out_specs, check_vma=False)
```

profile of v0, /device:TPU:2, one launch (start us, length us, event | category | flops | bytes accessed | tf_op | source)
XLA Modules:
  0.0 407.8 jit_solution(12967651325447050244)
XLA Ops:
  6.5 0.9 convert_reduce_fusion
  7.5 9.6 %all_to_all.39 = f32[4,1,1024]{2,1,0:T(1,128)S(1)} all-to-all(f32[4,1,1024]{2,1,0:T(1,128)S(1)} %broadcast_in_dim.122), channel_id=1, replica_groups=mesh['tile'=64,'mem'=4] {'mem'}, dimensions={0} | all-to-all | bytes 32768 | tf_op jit(solution)/shard_map/all_to_all | solution.py:13
  17.2 1.6 fusion.26
  19.8 1.6 gather_fusion.3
  21.5 0.7 all_to_all.25
  22.2 12.0 %all-to-all-start = ((s32[1,64,3]{2,0,1:T(1,128)}), s32[1,64,3]{2,0,1:T(1,128)S(1)}, u32[]{:S(2)}, u32[]{:S(2)}) async-start(s32[1,64,3]{2,0,1:T(1,128)} %bitcast), calls=%async_computation | async-start | bytes 65536 | tf_op jit(solution)/shard_map/all_to_all | solution.py:72
  35.6 66.0 %all-gather.2.cloned.1.call-done = bf16[64,65536]{1,0:T(8,128)(2,1)} async-done(((bf16[64,1024]{1,0:T(8,128)(2,1)}), bf16[64,65536]{1,0:T(8,128)(2,1)}) %all-gather.2.cloned.1.call-update) | async-done | bytes 8388624 | tf_op jit(solution)/shard_map/all_gather | solution.py:61
  101.5 9.0 %copy_bitcast_fusion = bf16[64,512,128]{2,0,1:T(8,128)(2,1)} fusion(bf16[64,65536]{1,0:T(8,128)(2,1)} %all-gather.2.cloned.1.call-done), kind=kLoop, calls=%fused_computation.7 | loop fusion | bytes 16777216 | tf_op jit(solution)/shard_map/reshape | solution.py:62
  110.5 5.5 %gather_fusion = bf16[128,64,128]{2,1,0:T(8,128)(2,1)} fusion(bf16[64,512,128]{2,0,1:T(8,128)(2,1)} %copy_bitcast_fusion, s32[1024]{0:T(1024)S(1)} %pad_clamp_fusion.3), kind=kCustom, calls=%fused_computation.4 | custom fusion | bytes 4194816 | tf_op jit(solution)/shard_map/jit(_take)/gather | solution.py:62
  116.1 5.8 %convolution_bitcast_fusion.1 = bf16[64,128,128]{2,0,1:T(8,128)(2,1)S(1)} fusion(bf16[128,128,128]{2,1,0:T(8,128)(2,1)} %param.10, bf16[128,64,128]{2,1,0:T(8,128)(2,1)} %gather_fusion, pred[128]{0:T(512)(128)(4,1)S(1)} %compare_and_fusion.2), kind=kOutput, calls=%fused_computation.18 | convolution fusion | flops 269484032 | bytes 8388736 | tf_op jit(solution)/shard_map/mtk,trk->mtr/dot_general | solution.py:63
  121.8 2.7 gather_fusion.4
  124.6 4.3 %fusion.1 = bf16[64,192,128]{2,0,1:T(8,128)(2,1)} fusion(bf16[192,64,128]{2,1,0:T(8,128)(2,1)} %gather_fusion.4, pred[192]{0:T(512)(128)(4,1)S(1)} %get-tuple-element.14, pred[192]{0:T(512)(128)(4,1)S(1)} %fusion.27), kind=kLoop, calls=%fused_computation.11 | loop fusion | flops 3145728 | bytes 6291840 | tf_op jit(solution)/shard_map/convert_element_type | solution.py:70
  128.8 7.8 %all-to-all-start.2 = ((bf16[64,192,128]{2,0,1:T(8,128)(2,1)}), bf16[64,192,128]{2,0,1:T(8,128)(2,1)S(1)}, u32[]{:S(2)}, u32[]{:S(2)}) async-start(bf16[64,192,128]{2,0,1:T(8,128)(2,1)} %fusion.1), calls=%async_computation.2 | async-start | bytes 6291456 | tf_op jit(solution)/shard_map/all_to_all | solution.py:69
  136.7 1.9 copy.34
  139.1 0.7 minimum_reduce_fusion
  140.2 70.2 %all-to-all-done.2 = bf16[64,192,128]{2,0,1:T(8,128)(2,1)S(1)} async-done(((bf16[64,192,128]{2,0,1:T(8,128)(2,1)}), bf16[64,192,128]{2,0,1:T(8,128)(2,1)S(1)}, u32[]{:S(2)}, u32[]{:S(2)}) %all-to-all-start.2) | async-done | bytes 3145760 | tf_op jit(solution)/shard_map/all_to_all | solution.py:69
  210.4 2.8 fusion.21
  213.3 1.2 gather_fusion.1
  214.5 2.1 select_bitcast_fusion
  216.6 5.4 %all-to-all-start.3 = ((bf16[64,192,128]{2,0,1:T(8,128)(2,1)}), bf16[64,192,128]{2,0,1:T(8,128)(2,1)S(1)}, u32[]{:S(2)}, u32[]{:S(2)}) async-start(bf16[64,192,128]{2,0,1:T(8,128)(2,1)} %select_bitcast_fusion), calls=%async_computation.3 | async-start | bytes 6291456 | tf_op jit(solution)/shard_map/all_to_all | solution.py:81
  222.3 1.6 gather_fusion.6
  224.0 0.8 all_to_all.31
  224.8 70.9 %all-to-all-done.3 = bf16[64,192,128]{2,0,1:T(8,128)(2,1)S(1)} async-done(((bf16[64,192,128]{2,0,1:T(8,128)(2,1)}), bf16[64,192,128]{2,0,1:T(8,128)(2,1)S(1)}, u32[]{:S(2)}, u32[]{:S(2)}) %all-to-all-start.3) | async-done | bytes 3145760 | tf_op jit(solution)/shard_map/all_to_all | solution.py:81
  295.8 5.4 %all-to-all-start.5 = ((s32[1,64,3]{2,0,1:T(1,128)}), s32[1,64,3]{2,0,1:T(1,128)S(1)}, u32[]{:S(2)}, u32[]{:S(2)}) async-start(s32[1,64,3]{2,0,1:T(1,128)} %bitcast.12), calls=%async_computation.5 | async-start | bytes 65536 | tf_op jit(solution)/shard_map/all_to_all | solution.py:92
  301.2 2.2 gather_fusion.2
  303.4 4.1 %convolution_bitcast_fusion = bf16[64,128,128]{2,0,1:T(8,128)(2,1)S(1)} fusion(bf16[128,128,128]{2,1,0:T(8,128)(2,1)} %param.10, bf16[128,64,128]{2,1,0:T(8,128)(2,1)} %gather_fusion.2, pred[128]{0:T(512)(128)(4,1)S(1)} %get-tuple-element.11), kind=kOutput, calls=%fused_computation.17 | convolution fusion | flops 269484032 | bytes 8388736 | tf_op jit(solution)/shard_map/mtr,trk->mtk/dot_general | solution.py:83
  307.5 2.7 gather_fusion.5
  310.2 4.3 %fusion = bf16[64,192,128]{2,0,1:T(8,128)(2,1)} fusion(bf16[192,64,128]{2,1,0:T(8,128)(2,1)} %gather_fusion.5, pred[192]{0:T(512)(128)(4,1)S(1)} %get-tuple-element.10, pred[192]{0:T(512)(128)(4,1)S(1)} %fusion.28), kind=kLoop, calls=%fused_computation.9 | loop fusion | flops 3145728 | bytes 6291840 | tf_op jit(solution)/shard_map/convert_element_type | solution.py:90
  314.5 10.3 %all-to-all-start.4 = ((bf16[64,192,128]{2,0,1:T(8,128)(2,1)}), bf16[64,192,128]{2,0,1:T(8,128)(2,1)S(1)}, u32[]{:S(2)}, u32[]{:S(2)}) async-start(bf16[64,192,128]{2,0,1:T(8,128)(2,1)} %fusion), calls=%async_computation.4 | async-start | bytes 6291456 | tf_op jit(solution)/shard_map/all_to_all | solution.py:89
  325.5 73.0 %all-to-all-done.4 = bf16[64,192,128]{2,0,1:T(8,128)(2,1)S(1)} async-done(((bf16[64,192,128]{2,0,1:T(8,128)(2,1)}), bf16[64,192,128]{2,0,1:T(8,128)(2,1)S(1)}, u32[]{:S(2)}, u32[]{:S(2)}) %all-to-all-start.4) | async-done | bytes 3145760 | tf_op jit(solution)/shard_map/all_to_all | solution.py:89
  398.5 1.7 fusion.2
  400.2 0.8 copy.50
  (39 shorter events, 4.6 us)
Async XLA Ops:
  6.5 95.0 %all-gather.2.cloned.1.call-start = ((), (), s32[]{:S(2)}) async-start(), calls=%async_computation.6 | async-start | bytes 8519680 | tf_op jit(solution)/shard_map/all_gather | solution.py:61
  22.2 106.6 %all-to-all-start = ((s32[1,64,3]{2,0,1:T(1,128)}), s32[1,64,3]{2,0,1:T(1,128)S(1)}, u32[]{:S(2)}, u32[]{:S(2)}) async-start(s32[1,64,3]{2,0,1:T(1,128)} %bitcast), calls=%async_computation | async-start | bytes 65536 | tf_op jit(solution)/shard_map/all_to_all | solution.py:72
  128.8 9.8 %copy-start = (s32[2048]{0:T(1024)S(1)}, s32[2048]{0:T(1024)}, u32[]{:S(2)}) copy-start(s32[2048]{0:T(1024)} %param.15) | copy-start | bytes 24580
  128.8 81.6 %all-to-all-start.2 = ((bf16[64,192,128]{2,0,1:T(8,128)(2,1)}), bf16[64,192,128]{2,0,1:T(8,128)(2,1)S(1)}, u32[]{:S(2)}, u32[]{:S(2)}) async-start(bf16[64,192,128]{2,0,1:T(8,128)(2,1)} %fusion.1), calls=%async_computation.2 | async-start | bytes 6291456 | tf_op jit(solution)/shard_map/all_to_all | solution.py:69
  216.6 79.2 %all-to-all-start.3 = ((bf16[64,192,128]{2,0,1:T(8,128)(2,1)}), bf16[64,192,128]{2,0,1:T(8,128)(2,1)S(1)}, u32[]{:S(2)}, u32[]{:S(2)}) async-start(bf16[64,192,128]{2,0,1:T(8,128)(2,1)} %select_bitcast_fusion), calls=%async_computation.3 | async-start | bytes 6291456 | tf_op jit(solution)/shard_map/all_to_all | solution.py:81
  295.8 18.7 %all-to-all-start.5 = ((s32[1,64,3]{2,0,1:T(1,128)}), s32[1,64,3]{2,0,1:T(1,128)S(1)}, u32[]{:S(2)}, u32[]{:S(2)}) async-start(s32[1,64,3]{2,0,1:T(1,128)} %bitcast.12), calls=%async_computation.5 | async-start | bytes 65536 | tf_op jit(solution)/shard_map/all_to_all | solution.py:92
  314.5 84.0 %all-to-all-start.4 = ((bf16[64,192,128]{2,0,1:T(8,128)(2,1)}), bf16[64,192,128]{2,0,1:T(8,128)(2,1)S(1)}, u32[]{:S(2)}, u32[]{:S(2)}) async-start(bf16[64,192,128]{2,0,1:T(8,128)(2,1)} %fusion), calls=%async_computation.4 | async-start | bytes 6291456 | tf_op jit(solution)/shard_map/all_to_all | solution.py:89
Sparse Core Ops, SparseCore 0:
  18.9 82.6 all-gather.1
where the time goes:
time: 409 us; the launch traced here: 408 us
  waiting for transfers between devices  280 us (68%)
  starting transfers between devices  41 us (10%)
  local copies, waits for them, and re-layouts  31.6 us (8%)
  other arithmetic  17.4 us (4%)
  matrix products  14.4 us (4%)
  between operations  13.6 us (3%)
  blocking collectives  9.63 us (2%)
    all_to_all x1, waiting for transfers between devices, body(): lax.all_to_all(sent_back.astype(jnp.bfloat16), 'tile', split_axis=1, conc...  73 us
    all_to_all x1, waiting for transfers between devices, body(): lax.all_to_all(reply_rows, 'tile', split_axis=1, concat_axis=1, tiled=True)  70.9 us
    all_to_all x1, waiting for transfers between devices, body(): lax.all_to_all(sent_terms.astype(jnp.bfloat16), 'tile', split_axis=1, con...  70.2 us
    all_gather x1, waiting for transfers between devices, body(): gathered = lax.all_gather(member_deviations, 'tile', axis=1, tiled=True)  66 us
    all_to_all x1, starting transfers between devices, body(): lax.all_to_all(row_index[None, :], 'tile', split_axis=1, concat_axis=1, t...  12 us
    all_to_all x1, starting transfers between devices, body(): lax.all_to_all(sent_back.astype(jnp.bfloat16), 'tile', split_axis=1, conc...  10.3 us
    all_to_all x1, blocking collectives, sent_to_all(): lax.all_to_all(jnp.broadcast_to(value[None], (size, *value.shape)), axis,...  9.63 us
    reshape x1, local copies, waits for them, and re-layouts, body(): gathered.reshape(local_members, -1, tile_size)  9.01 us
  transfers between devices with their start and end apart: 6, of which 4 were waited for; matrix products, arithmetic and copies ran while one was open for 12% of the time, Pallas kernels for 0%

commit v1 on v0

--- a/solution.py
+++ b/solution.py
@@ -58,7 +58,10 @@
     col_slot = slot_of(col_owner, capacity)
     row_source, row_used = invert(row_slot, slot_total)
     col_source, col_used = invert(col_slot, slot_total)
-    gathered = lax.all_gather(member_deviations, "tile", axis=1, tiled=True)
+    peers = lax.axis_size("tile")
+    blocks = jnp.stack([member_deviations for _ in range(peers)])
+    blocks = lax.all_to_all(blocks, "tile", split_axis=0, concat_axis=0)
+    gathered = jnp.concatenate(blocks, axis=1)
     retrieved_blocks = jnp.take(gathered.reshape(local_members, -1, tile_size), tile_col, axis=1)
     forward_terms = jnp.einsum(
         "mtk,trk->mtr", retrieved_blocks, footprints, preferred_element_type=jnp.float32

time: 409 us -> 551 us (1.35)
  waiting for transfers between devices: 280 us -> 396 us
  local copies, waits for them, and re-layouts: 31.6 us -> 63.5 us
  between operations: 13.6 us -> 0.27 us
  starting transfers between devices: 41 us -> 51.3 us
    all_to_all x0 -> x1, waiting for transfers between devices: none -> 182 us  [body(): blocks = lax.all_to_all(blocks, 'tile', split_axis=0, concat_axis=0)]
    all_gather x1 -> x0, waiting for transfers between devices: 66 us -> none  [body(): gathered = lax.all_gather(member_deviations, 'tile', axis=1, tiled=True)]
    another operation x0 -> x3, local copies, waits for them, and re-layouts: none -> 29.6 us  [the longest x2 25.3 us: body(): gathered.reshape(local_members, -1, tile_size)]
    all_to_all x0 -> x1, starting transfers between devices: none -> 12.3 us  [body(): blocks = lax.all_to_all(blocks, 'tile', split_axis=0, concat_axis=0)]
  transfers between devices with their start and end apart: 6 -> 6, of which waited for: 4 -> 4; matrix products, arithmetic and copies ran while one was open for 12% -> 14% of each run, Pallas kernels for 0% -> 0%
where the time goes in v1:
time: 551 us; the launch traced here: 550 us
  waiting for transfers between devices  396 us (72%)
  local copies, waits for them, and re-layouts  63.5 us (12%)
  starting transfers between devices  51.3 us (9%)
  other arithmetic  14.8 us (3%)
  matrix products  14.4 us (3%)
  blocking collectives  9.63 us (2%)
    all_to_all x1, waiting for transfers between devices, body(): blocks = lax.all_to_all(blocks, 'tile', split_axis=0, concat_axis=0)  182 us
    all_to_all x1, waiting for transfers between devices, body(): lax.all_to_all(sent_back.astype(jnp.bfloat16), 'tile', split_axis=1, conc...  73 us
    all_to_all x1, waiting for transfers between devices, body(): lax.all_to_all(reply_rows, 'tile', split_axis=1, concat_axis=1, tiled=True)  70.9 us
    all_to_all x1, waiting for transfers between devices, body(): lax.all_to_all(sent_terms.astype(jnp.bfloat16), 'tile', split_axis=1, con...  70.2 us
    another operation x2, local copies, waits for them, and re-layouts, body(): gathered.reshape(local_members, -1, tile_size)  25.3 us
    all_to_all x1, starting transfers between devices, body(): blocks = lax.all_to_all(blocks, 'tile', split_axis=0, concat_axis=0)  12.3 us
    reshape x1, local copies, waits for them, and re-layouts, body(): gathered = jnp.concatenate(blocks, axis=1)  11.3 us
  transfers between devices with their start and end apart: 6, of which 4 were waited for; matrix products, arithmetic and copies ran while one was open for 14% of the time, Pallas kernels for 0%

profile of v1, /device:TPU:2, one launch (start us, length us, event | category | flops | bytes accessed | tf_op | source)
XLA Modules:
  0.0 550.3 jit_solution(1539384801928295491)
XLA Ops:
  0.0 0.9 convert_reduce_fusion
  1.0 9.6 %all_to_all.44 = f32[4,1,1024]{2,1,0:T(1,128)S(1)} all-to-all(f32[4,1,1024]{2,1,0:T(1,128)S(1)} %broadcast_in_dim.122), channel_id=1, replica_groups=mesh['tile'=64,'mem'=4] {'mem'}, dimensions={0} | all-to-all | bytes 32768 | tf_op jit(solution)/shard_map/all_to_all | solution.py:13
  10.6 0.9 fusion.26
  11.6 4.3 stack.2
  15.8 12.3 %all-to-all-start.2 = ((bf16[64,64,1024]{2,1,0:T(8,128)(2,1)}), bf16[64,64,1024]{2,1,0:T(8,128)(2,1)}, u32[]{:S(2)}, u32[]{:S(2)}) async-start(bf16[64,64,1024]{2,1,0:T(8,128)(2,1)} %stack.2), calls=%async_computation.2 | async-start | bytes 16777216 | tf_op jit(solution)/shard_map/all_to_all | solution.py:63
  28.5 1.6 gather_fusion.3
  31.0 182.2 %all-to-all-done.2 = bf16[64,64,1024]{2,1,0:T(8,128)(2,1)} async-done(((bf16[64,64,1024]{2,1,0:T(8,128)(2,1)}), bf16[64,64,1024]{2,1,0:T(8,128)(2,1)}, u32[]{:S(2)}, u32[]{:S(2)}) %all-to-all-start.2) | async-done | bytes 8388640 | tf_op jit(solution)/shard_map/all_to_all | solution.py:63
  213.2 7.4 %all-to-all-start = ((s32[1,64,3]{2,0,1:T(1,128)}), s32[1,64,3]{2,0,1:T(1,128)S(1)}, u32[]{:S(2)}, u32[]{:S(2)}) async-start(s32[1,64,3]{2,0,1:T(1,128)} %bitcast), calls=%async_computation | async-start | bytes 65536 | tf_op jit(solution)/shard_map/all_to_all | solution.py:75
  220.6 11.3 %copy.30 = bf16[64,64,1024]{2,1,0:T(8,128)(2,1)} copy(bf16[64,64,1024]{2,0,1:T(8,128)(2,1)} %bitcast.2) | data formatting | bytes 16777216 | tf_op jit(solution)/shard_map/reshape | solution.py:64
  231.9 13.3 %reshape_reshape.3 = bf16[64,512,128]{2,1,0:T(8,128)(2,1)} reshape(bf16[64,64,1024]{2,1,0:T(8,128)(2,1)} %copy.30) | data formatting | bytes 16777216 | tf_op jit(solution)/shard_map/reshape;reshape | solution.py:65
  245.2 12.0 %copy.31 = bf16[64,512,128]{2,0,1:T(8,128)(2,1)} copy(bf16[64,512,128]{2,1,0:T(8,128)(2,1)} %reshape_reshape.3) | data formatting | bytes 16777216 | tf_op jit(solution)/shard_map/reshape;reshape | solution.py:65
  257.2 5.5 %gather_fusion = bf16[128,64,128]{2,1,0:T(8,128)(2,1)} fusion(bf16[64,512,128]{2,0,1:T(8,128)(2,1)} %copy.31, s32[1024]{0:T(1024)S(1)} %pad_clamp_fusion.3), kind=kCustom, calls=%fused_computation.4 | custom fusion | bytes 4194816 | tf_op jit(solution)/shard_map/jit(_take)/gather | solution.py:65
  262.8 5.8 %convolution_bitcast_fusion.1 = bf16[64,128,128]{2,0,1:T(8,128)(2,1)S(1)} fusion(bf16[128,128,128]{2,1,0:T(8,128)(2,1)} %param.10, bf16[128,64,128]{2,1,0:T(8,128)(2,1)} %gather_fusion, pred[128]{0:T(512)(128)(4,1)S(1)} %compare_and_fusion.2), kind=kOutput, calls=%fused_computation.17 | convolution fusion | flops 269484032 | bytes 8388736 | tf_op jit(solution)/shard_map/mtk,trk->mtr/dot_general | solution.py:66
  268.5 2.7 gather_fusion.4
  271.2 4.3 fusion.1
  275.5 10.4 %all-to-all-start.3 = ((bf16[64,192,128]{2,0,1:T(8,128)(2,1)}), bf16[64,192,128]{2,0,1:T(8,128)(2,1)S(1)}, u32[]{:S(2)}, u32[]{:S(2)}) async-start(bf16[64,192,128]{2,0,1:T(8,128)(2,1)} %fusion.1), calls=%async_computation.3 | async-start | bytes 6291456 | tf_op jit(solution)/shard_map/all_to_all | solution.py:72
  286.0 1.9 copy.37
  289.5 70.2 %all-to-all-done.3 = bf16[64,192,128]{2,0,1:T(8,128)(2,1)S(1)} async-done(((bf16[64,192,128]{2,0,1:T(8,128)(2,1)}), bf16[64,192,128]{2,0,1:T(8,128)(2,1)S(1)}, u32[]{:S(2)}, u32[]{:S(2)}) %all-to-all-start.3) | async-done | bytes 3145760 | tf_op jit(solution)/shard_map/all_to_all | solution.py:72
  359.7 2.8 fusion.21
  362.6 1.2 gather_fusion.1
  363.8 2.1 select_bitcast_fusion
  365.8 5.4 all-to-all-start.4
  371.6 1.6 gather_fusion.6
  374.1 70.9 %all-to-all-done.4 = bf16[64,192,128]{2,0,1:T(8,128)(2,1)S(1)} async-done(((bf16[64,192,128]{2,0,1:T(8,128)(2,1)}), bf16[64,192,128]{2,0,1:T(8,128)(2,1)S(1)}, u32[]{:S(2)}, u32[]{:S(2)}) %all-to-all-start.4) | async-done | bytes 3145760 | tf_op jit(solution)/shard_map/all_to_all | solution.py:84
  445.0 5.4 all-to-all-start.6
  450.5 2.2 gather_fusion.2
  452.6 4.1 convolution_bitcast_fusion
  456.7 2.7 gather_fusion.5
  459.5 4.3 fusion
  463.7 10.3 %all-to-all-start.5 = ((bf16[64,192,128]{2,0,1:T(8,128)(2,1)}), bf16[64,192,128]{2,0,1:T(8,128)(2,1)S(1)}, u32[]{:S(2)}, u32[]{:S(2)}) async-start(bf16[64,192,128]{2,0,1:T(8,128)(2,1)} %fusion), calls=%async_computation.5 | async-start | bytes 6291456 | tf_op jit(solution)/shard_map/all_to_all | solution.py:92
  474.8 73.0 %all-to-all-done.5 = bf16[64,192,128]{2,0,1:T(8,128)(2,1)S(1)} async-done(((bf16[64,192,128]{2,0,1:T(8,128)(2,1)}), bf16[64,192,128]{2,0,1:T(8,128)(2,1)S(1)}, u32[]{:S(2)}, u32[]{:S(2)}) %all-to-all-start.5) | async-done | bytes 3145760 | tf_op jit(solution)/shard_map/all_to_all | solution.py:92
  547.8 1.7 fusion.2
  (45 shorter events, 5.6 us)
Async XLA Ops:
  15.8 12.4 %copy-start.2 = (s32[128]{0:T(128)S(1)}, s32[128]{0:T(128)}, u32[]{:S(2)}) copy-start(s32[128]{0:T(128)} %param.11) | copy-start | bytes 1540
  15.8 15.2 %copy-start.1 = (s32[128]{0:T(128)S(1)}, s32[128]{0:T(128)}, u32[]{:S(2)}) copy-start(s32[128]{0:T(128)} %param.12) | copy-start | bytes 1540
  15.8 197.4 %all-to-all-start.2 = ((bf16[64,64,1024]{2,1,0:T(8,128)(2,1)}), bf16[64,64,1024]{2,1,0:T(8,128)(2,1)}, u32[]{:S(2)}, u32[]{:S(2)}) async-start(bf16[64,64,1024]{2,1,0:T(8,128)(2,1)} %stack.2), calls=%async_computation.2 | async-start | bytes 16777216 | tf_op jit(solution)/shard_map/all_to_all | solution.py:63
  213.2 62.3 %all-to-all-start = ((s32[1,64,3]{2,0,1:T(1,128)}), s32[1,64,3]{2,0,1:T(1,128)S(1)}, u32[]{:S(2)}, u32[]{:S(2)}) async-start(s32[1,64,3]{2,0,1:T(1,128)} %bitcast), calls=%async_computation | async-start | bytes 65536 | tf_op jit(solution)/shard_map/all_to_all | solution.py:75
  275.5 12.4 %copy-start = (s32[2048]{0:T(1024)S(1)}, s32[2048]{0:T(1024)}, u32[]{:S(2)}) copy-start(s32[2048]{0:T(1024)} %param.15) | copy-start | bytes 24580
  275.5 84.2 %all-to-all-start.3 = ((bf16[64,192,128]{2,0,1:T(8,128)(2,1)}), bf16[64,192,128]{2,0,1:T(8,128)(2,1)S(1)}, u32[]{:S(2)}, u32[]{:S(2)}) async-start(bf16[64,192,128]{2,0,1:T(8,128)(2,1)} %fusion.1), calls=%async_computation.3 | async-start | bytes 6291456 | tf_op jit(solution)/shard_map/all_to_all | solution.py:72
  365.8 79.2 %all-to-all-start.4 = ((bf16[64,192,128]{2,0,1:T(8,128)(2,1)}), bf16[64,192,128]{2,0,1:T(8,128)(2,1)S(1)}, u32[]{:S(2)}, u32[]{:S(2)}) async-start(bf16[64,192,128]{2,0,1:T(8,128)(2,1)} %select_bitcast_fusion), calls=%async_computation.4 | async-start | bytes 6291456 | tf_op jit(solution)/shard_map/all_to_all | solution.py:84
  445.0 18.7 %all-to-all-start.6 = ((s32[1,64,3]{2,0,1:T(1,128)}), s32[1,64,3]{2,0,1:T(1,128)S(1)}, u32[]{:S(2)}, u32[]{:S(2)}) async-start(s32[1,64,3]{2,0,1:T(1,128)} %bitcast.13), calls=%async_computation.6 | async-start | bytes 65536 | tf_op jit(solution)/shard_map/all_to_all | solution.py:95
  463.7 84.0 %all-to-all-start.5 = ((bf16[64,192,128]{2,0,1:T(8,128)(2,1)}), bf16[64,192,128]{2,0,1:T(8,128)(2,1)S(1)}, u32[]{:S(2)}, u32[]{:S(2)}) async-start(bf16[64,192,128]{2,0,1:T(8,128)(2,1)} %fusion), calls=%async_computation.5 | async-start | bytes 6291456 | tf_op jit(solution)/shard_map/all_to_all | solution.py:92
